TPU v7x, 32 devices: a whole 2x2x4 slice. The times are simulated.
32 devices in a mesh: row: 16 (over z, x, core), col: 2 (over y).
Axes of the slice: x: 2, y: 2, z: 4, core: 2. Of those that a mesh axis runs over, the one named last changes fastest.
Arguments:
- token_ids: int32 [512], P('col'), may hold values from 0 to 50559, as said below
- table: bfloat16 [50560, 5120], P('row', 'col'), may hold values from -120 to 120
- norm_gain: float32 [5120], replicated, may hold values from 0.5 to 1.5
- w_qkv: bfloat16 [5120, 7168], P('col', 'row'), may hold values from -0.078125 to 0.078125
- w_gate: bfloat16 [5120, 16384], P('col', 'row'), may hold values from -0.078125 to 0.078125
- w_up: bfloat16 [5120, 16384], P('col', 'row'), may hold values from -0.078125 to 0.078125
Outputs:
- qkv_out: bfloat16 [512, 7168], P('col', 'row')
- hidden: bfloat16 [512, 16384], P('col', 'row')
Inputs may be any that keep to these rules, and one draw needn't show every extreme that they name: `token_ids`: most ids of the micro-batch lie in one block of 3160 entries that starts at a multiple of 3160, which block being drawn; the others lie in the other blocks.
All inputs are finite; a program needn't handle non-finite values.
Results may differ from a plain program's by a relative error of at most 0.0058.
Values may be sent and summed in bfloat16 or wider, within the bound.
A program may use at most 128 MiB of HBM per device.

v0:
```python
import math
import jax
import jax.numpy as jnp
from jax import lax
from jax.sharding import PartitionSpec as P

eps = 1e-05


def lookup_partial(every_id, table_tile, vocab_first):
    total_rows = every_id.shape[0]
    block_rows = math.gcd(total_rows, 512)
    columns = vocab_first + lax.broadcasted_iota(jnp.int32, (1, table_tile.shape[0]), 1)

    def one_block(block_ids):
        onehot = (block_ids[:, None] == columns).astype(jnp.bfloat16)
        return jnp.dot(onehot, table_tile, preferred_element_type=jnp.float32).astype(jnp.bfloat16)

    pieces_out = lax.map(one_block, every_id.reshape(total_rows // block_rows, block_rows))
    return pieces_out.reshape(total_rows, table_tile.shape[1])


def body(token_ids, table, norm_gain, w_qkv, w_gate, w_up):
    every_id = lax.all_gather(token_ids, "col", axis=0, tiled=True)
    vocab_rows = table.shape[0]
    partial_value = lookup_partial(every_id, table, lax.axis_index("row") * vocab_rows)
    embedded = lax.psum(partial_value, "row").astype(jnp.float32).astype(jnp.bfloat16)
    token_rows = lax.all_to_all(embedded, "col", split_axis=0, concat_axis=1, tiled=True)
    values = token_rows.astype(jnp.float32)
    factor = lax.rsqrt(jnp.mean(values * values, axis=1, keepdims=True) + eps)
    normed = (values * factor * norm_gain[None, :]).astype(jnp.bfloat16)
    pieces = (
        lax.all_gather(w_qkv, "col", axis=0, tiled=True),
        lax.all_gather(w_gate, "col", axis=0, tiled=True),
        lax.all_gather(w_up, "col", axis=0, tiled=True),
    )
    qkv_total, gate_total, up_total = tuple(
        (jnp.dot(normed, piece, preferred_element_type=jnp.float32) for piece in pieces)
    )
    qkv_out = qkv_total.astype(jnp.bfloat16)
    hidden = (jax.nn.silu(gate_total) * up_total).astype(jnp.bfloat16)
    return (qkv_out, hidden)


def solution(mesh):
    return jax.shard_map(
        body,
        mesh=mesh,
        in_specs=(
            P("col"),
            P("row", "col"),
            P(),
            P("col", "row"),
            P("col", "row"),
            P("col", "row"),
        ),
        out_specs=(P("col", "row"), P("col", "row")),
        check_vma=False,
    )
```

profile of v0, /device:TPU:0, one launch (start us, length us, event | category | flops | bytes accessed | tf_op | source)
XLA Modules:
  0.0 398.8 jit_solution(8804500506668590405)
XLA Ops:
  8.0 0.0 all-reduce.2.cloned.1.call-start
  8.1 5.4 %all-gather = s32[2,1,256]{2,1,0:T(1,128)S(1)} all-gather(s32[1,1,256]{2,1,0:T(1,128)} %bitcast.20), channel_id=1, replica_groups=mesh['row'=16,'col'=2] {'col'}, dimensions={0}, use_global_device_ids=true | all-gather | bytes 3072 | tf_op jit(solution)/shard_map/all_gather | solution.py:24
  13.5 12.5 %fusion.4 = bf16[512,2560]{1,0:T(8,128)(2,1)S(1)} fusion(bf16[3160,2560]{1,0:T(8,128)(2,1)} %param.7, s32[3160]{0:T(1024)S(1)} %iota_add_fusion, s32[512]{0:T(512)S(1)} %bitcast.19), kind=kOutput, calls=%fused_computation.6 | convolution fusion | flops 8286679040 | bytes 18815328 | tf_op jit(solution)/shard_map/while/body/eval_jaxpr/dot_general | solution.py:17
  26.1 2.6 copy.9
  28.6 0.0 all-reduce.2.cloned.1.call-update
  28.6 0.0 all-gather.5.cloned.1.call-start
  28.7 0.5 all-gather.5.cloned.1.call-update
  29.2 0.0 all-gather.7.cloned.1.call-start
  29.3 0.5 all-gather.7.cloned.1.call-update
  29.8 0.0 all-gather.9.cloned.1.call-start
  29.9 0.5 all-gather.9.cloned.1.call-update
  30.4 0.0 copy-start
  30.4 100.8 %all-reduce.2.cloned.1.call-done = bf16[2,256,2560]{1,2,0:T(8,128)(2,1)} async-done(((bf16[2,256,2560]{1,2,0:T(8,128)(2,1)}), bf16[2,256,2560]{1,2,0:T(8,128)(2,1)}) %all-reduce.2.cloned.1.call-update) | async-done | bytes 2621456 | tf_op jit(solution)/shard_map/psum | solution.py:27
  131.2 63.0 %all_to_all.13 = bf16[2,256,2560]{1,2,0:T(8,128)(2,1)S(1)} all-to-all(bf16[2,256,2560]{1,2,0:T(8,128)(2,1)} %all-reduce.2.cloned.1.call-done), channel_id=1, replica_groups=mesh['row'=16,'col'=2] {'col'}, dimensions={0} | all-to-all | bytes 5242880 | tf_op jit(solution)/shard_map/all_to_all | solution.py:28
  194.1 0.7 multiply_reduce_fusion
  194.9 0.0 copy-done
  194.9 2.2 fusion.3
  197.1 0.0 all-gather.5.cloned.1.call-done
  197.1 4.3 %convolution_convert_fusion = bf16[256,448]{0,1:T(8,128)(2,1)} fusion(bf16[5120,448]{0,1:T(8,128)(2,1)} %all-gather.5.cloned.1.call-done, bf16[256,5120]{0,1:T(8,128)(2,1)S(1)} %fusion.3), kind=kOutput, calls=%fused_computation.11 | convolution fusion | flops 1174519808 | bytes 7438336 | tf_op jit(solution)/shard_map/dot_general | solution.py:38
  201.4 51.0 %all-gather.7.cloned.1.call-done = bf16[5120,1024]{1,0:T(8,128)(2,1)} async-done(((bf16[2560,1024]{1,0:T(8,128)(2,1)}), bf16[5120,1024]{1,0:T(8,128)(2,1)}) %all-gather.7.cloned.1.call-update) | async-done | bytes 10485776 | tf_op jit(solution)/shard_map/all_gather | solution.py:34
  252.4 7.8 %fusion.10 = f32[256,1024]{1,0:T(8,128)} fusion(bf16[256,5120]{0,1:T(8,128)(2,1)S(1)} %fusion.3, bf16[5120,1024]{1,0:T(8,128)(2,1)} %all-gather.7.cloned.1.call-done), kind=kOutput, calls=%fused_computation.14 | convolution fusion | flops 2684354560 | bytes 14155776 | tf_op jit(solution)/shard_map/dot_general | solution.py:38
  260.2 123.0 %all-gather.9.cloned.1.call-done = bf16[5120,1024]{1,0:T(8,128)(2,1)} async-done(((bf16[2560,1024]{1,0:T(8,128)(2,1)}), bf16[5120,1024]{1,0:T(8,128)(2,1)}) %all-gather.9.cloned.1.call-update) | async-done | bytes 10485776 | tf_op jit(solution)/shard_map/all_gather | solution.py:35
  383.2 8.0 %fusion.9 = bf16[256,1024]{1,0:T(8,128)(2,1)} fusion(bf16[256,5120]{0,1:T(8,128)(2,1)S(1)} %fusion.3, bf16[5120,1024]{1,0:T(8,128)(2,1)} %all-gather.9.cloned.1.call-done, f32[256,1024]{1,0:T(8,128)} %fusion.10), kind=kOutput, calls=%fused_computation.10 | convolution fusion | flops 2685927424 | bytes 14680064 | tf_op jit(solution)/shard_map/dot_general | solution.py:38
  (2 shorter events, 0.0 us)
Async XLA Ops:
  8.0 123.2 %all-reduce.2.cloned.1.call-start = ((), (), s32[]{:S(2)}) async-start(), calls=%async_computation.1 | async-start | bytes 5242880 | tf_op jit(solution)/shard_map/psum | solution.py:27
  28.6 168.4 %all-gather.5.cloned.1.call-start = ((), (), s32[]{:S(2)}) async-start(), calls=%async_computation.2 | async-start | bytes 6881280 | tf_op jit(solution)/shard_map/all_gather | solution.py:33
  29.2 223.2 %all-gather.7.cloned.1.call-start = ((), (), s32[]{:S(2)}) async-start(), calls=%async_computation.3 | async-start | bytes 15728640 | tf_op jit(solution)/shard_map/all_gather | solution.py:34
  29.8 353.4 %all-gather.9.cloned.1.call-start = ((), (), s32[]{:S(2)}) async-start(), calls=%async_computation.4 | async-start | bytes 15728640 | tf_op jit(solution)/shard_map/all_gather | solution.py:35
  30.4 164.5 %copy-start = (f32[5120]{0:T(1024)S(1)}, f32[5120]{0:T(1024)}, u32[]{:S(2)}) copy-start(f32[5120]{0:T(1024)} %param.8) | copy-start | bytes 61444
Sparse Core Ops, SparseCore 0:
  28.8 102.3 all-reduce.1
Sparse Core Ops, SparseCore 1:
  30.7 62.7 all-gather.4
  94.9 157.4 all-gather.6
  253.8 129.3 all-gather.8
where the time goes:
time: 399 us
  waiting for transfers between devices  276 us (69%)
  blocking collectives  68.4 us (17%)
  matrix products  32.7 us (8%)
  between operations  15.7 us (4%)
    all_gather x1, waiting for transfers between devices, body(): lax.all_gather(w_up, 'col', axis=0, tiled=True)  123 us
    psum x1, waiting for transfers between devices, body(): lax.psum(partial_value, 'row').astype(jnp.float32).astype(jnp.bfloat16)  101 us
    all_to_all x1, blocking collectives, body(): lax.all_to_all(embedded, 'col', split_axis=0, concat_axis=1, tiled=True)  63 us
    all_gather x1, waiting for transfers between devices, body(): lax.all_gather(w_gate, 'col', axis=0, tiled=True)  51 us
    dot_general x3, matrix products, body(): jnp.dot(normed, piece, preferred_element_type=jnp.float32)  20.2 us
    dot_general x1, matrix products, one_block(): jnp.dot(onehot, table_tile, preferred_element_type=jnp.float32)  12.5 us
  transfers between devices with their start and end apart: 4, of which 3 were waited for; matrix products, arithmetic and copies ran while one was open for 4% of the time, Pallas kernels for 0%

commit v1 on v0

--- a/solution.py
+++ b/solution.py
@@ -5,6 +5,27 @@
 from jax.sharding import PartitionSpec as P
 
 eps = 1e-05
+
+
+def in_order(parts, dim):
+    shape = list(parts.shape[1:])
+    shape[dim] *= parts.shape[0]
+    return jnp.moveaxis(parts, 0, dim).reshape(shape)
+
+
+def collected_by_bits(value, axis):
+    length, mine = (lax.axis_size(axis), lax.axis_index(axis))
+    blocks, bit = (value[None], 1)
+    while bit < length:
+        other = lax.ppermute(blocks, axis, [(i, i ^ bit) for i in range(length)])
+        low = mine & bit == 0
+        blocks = jnp.concatenate([jnp.where(low, blocks, other), jnp.where(low, other, blocks)])
+        bit *= 2
+    return blocks
+
+
+def doubled_up(value, axis, dim):
+    return in_order(collected_by_bits(value, axis), dim)
 
 
 def lookup_partial(every_id, table_tile, vocab_first):
@@ -32,7 +53,7 @@
     pieces = (
         lax.all_gather(w_qkv, "col", axis=0, tiled=True),
         lax.all_gather(w_gate, "col", axis=0, tiled=True),
-        lax.all_gather(w_up, "col", axis=0, tiled=True),
+        doubled_up(w_up, "col", 0),
     )
     qkv_total, gate_total, up_total = tuple(
         (jnp.dot(normed, piece, preferred_element_type=jnp.float32) for piece in pieces)

time: 399 us -> 353 us (0.88)
  blocking collectives: 68.4 us -> 5.44 us
  other arithmetic: 2.91 us -> 12.7 us
  starting transfers between devices: 0.16 us -> 6.2 us
  waiting for transfers between devices: 276 us -> 281 us
  matrix products: 32.7 us -> 28.2 us
    all_to_all x0 -> x1, waiting for transfers between devices: none -> 149 us  [body(): lax.all_to_all(embedded, 'col', split_axis=0, concat_axis=1, tiled=True)]
    all_gather x1 -> x0, waiting for transfers between devices: 123 us -> none  [body(): lax.all_gather(w_up, 'col', axis=0, tiled=True)]
    all_to_all x1 -> x0, blocking collectives: 63 us -> none  [body(): lax.all_to_all(embedded, 'col', split_axis=0, concat_axis=1, tiled=True)]
    all_gather x1, waiting for transfers between devices: 51 us -> 31.5 us  [body(): lax.all_gather(w_gate, 'col', axis=0, tiled=True)]
    select_n x0 -> x1, other arithmetic: none -> 8.69 us  [collected_by_bits(): jnp.where(low, blocks, other)]
    dot_general x3, matrix products: 20.2 us -> 15.6 us  [body(): jnp.dot(normed, piece, preferred_element_type=jnp.float32)]
    all_to_all x0 -> x1, starting transfers between devices: none -> 4.03 us  [body(): lax.all_to_all(embedded, 'col', split_axis=0, concat_axis=1, tiled=True)]
  transfers between devices with their start and end apart: 4 -> 5, of which waited for: 3 -> 3; matrix products, arithmetic and copies ran while one was open for 4% -> 5% of each run, Pallas kernels for 0% -> 0%
where the time goes in v1:
time: 353 us
  waiting for transfers between devices  281 us (80%)
  matrix products  28.2 us (8%)
  between operations  15.5 us (4%)
  other arithmetic  12.7 us (4%)
  starting transfers between devices  6.2 us (2%)
  blocking collectives  5.44 us (2%)
  local copies, waits for them, and re-layouts  3.96 us (1%)
    all_to_all x1, waiting for transfers between devices, body(): lax.all_to_all(embedded, 'col', split_axis=0, concat_axis=1, tiled=True)  149 us
    psum x1, waiting for transfers between devices, body(): lax.psum(partial_value, 'row').astype(jnp.float32).astype(jnp.bfloat16)  99.4 us
    all_gather x1, waiting for transfers between devices, body(): lax.all_gather(w_gate, 'col', axis=0, tiled=True)  31.5 us
    dot_general x3, matrix products, body(): jnp.dot(normed, piece, preferred_element_type=jnp.float32)  15.6 us
    dot_general x1, matrix products, one_block(): jnp.dot(onehot, table_tile, preferred_element_type=jnp.float32)  12.5 us
    select_n x1, other arithmetic, collected_by_bits(): jnp.where(low, blocks, other)  8.69 us
  transfers between devices with their start and end apart: 5, of which 3 were waited for; matrix products, arithmetic and copies ran while one was open for 5% of the time, Pallas kernels for 0%

profile of v1, /device:TPU:0, one launch (start us, length us, event | category | flops | bytes accessed | tf_op | source)
XLA Modules:
  0.0 353.1 jit_solution(15200671035809601756)
XLA Ops:
  8.0 0.0 all-reduce.2.cloned.1.call-start
  8.0 5.4 %all-gather = s32[2,1,256]{2,1,0:T(1,128)S(1)} all-gather(s32[1,1,256]{2,1,0:T(1,128)} %bitcast.37), channel_id=1, replica_groups=mesh['row'=16,'col'=2] {'col'}, dimensions={0}, use_global_device_ids=true | all-gather | bytes 3072 | tf_op jit(solution)/shard_map/all_gather | solution.py:45
  13.5 12.5 %fusion.8 = bf16[512,2560]{1,0:T(8,128)(2,1)S(1)} fusion(bf16[3160,2560]{1,0:T(8,128)(2,1)} %param.7, s32[3160]{0:T(1024)S(1)} %iota_add_fusion, s32[512]{0:T(512)S(1)} %bitcast.36), kind=kOutput, calls=%fused_computation.13 | convolution fusion | flops 8286679040 | bytes 18815328 | tf_op jit(solution)/shard_map/while/body/eval_jaxpr/dot_general | solution.py:38
  26.1 2.7 copy.10
  28.7 0.0 all-reduce.2.cloned.1.call-update
  28.7 0.0 all-gather.4.cloned.1.call-start
  28.8 0.5 all-gather.4.cloned.1.call-update
  29.3 0.0 copy-start.2
  29.3 0.0 all-gather.6.cloned.1.call-start
  29.4 0.5 all-gather.6.cloned.1.call-update
  29.9 2.0 collective-permute-start
  32.0 99.4 %all-reduce.2.cloned.1.call-done = bf16[2,256,2560]{1,2,0:T(8,128)(2,1)} async-done(((bf16[2,256,2560]{1,2,0:T(8,128)(2,1)}), bf16[2,256,2560]{1,2,0:T(8,128)(2,1)}) %all-reduce.2.cloned.1.call-update) | async-done | bytes 2621456 | tf_op jit(solution)/shard_map/psum | solution.py:48
  131.4 4.0 %all-to-all-start = ((bf16[2,256,2560]{1,2,0:T(8,128)(2,1)}), bf16[2,256,2560]{1,2,0:T(8,128)(2,1)S(1)}, u32[]{:S(2)}, u32[]{:S(2)}) async-start(bf16[2,256,2560]{1,2,0:T(8,128)(2,1)} %all-reduce.2.cloned.1.call-done), calls=%async_computation | async-start | bytes 5242880 | tf_op jit(solution)/shard_map/all_to_all | solution.py:49
  135.4 0.0 copy-done.2
  135.5 149.1 %all-to-all-done = bf16[2,256,2560]{1,2,0:T(8,128)(2,1)S(1)} async-done(((bf16[2,256,2560]{1,2,0:T(8,128)(2,1)}), bf16[2,256,2560]{1,2,0:T(8,128)(2,1)S(1)}, u32[]{:S(2)}, u32[]{:S(2)}) %all-to-all-start) | async-done | bytes 2621472 | tf_op jit(solution)/shard_map/all_to_all | solution.py:49
  284.5 0.7 multiply_reduce_fusion
  285.2 3.2 fusion.7
  288.5 0.0 all-gather.4.cloned.1.call-done
  288.5 5.2 %convolution_convert_fusion = bf16[256,448]{0,1:T(8,128)(2,1)} fusion(bf16[5120,448]{0,1:T(8,128)(2,1)} %all-gather.4.cloned.1.call-done, bf16[256,5120]{0,1:T(8,128)(2,1)} %fusion.7), kind=kOutput, calls=%fused_computation.23 | convolution fusion | flops 1174519808 | bytes 7438336 | tf_op jit(solution)/shard_map/dot_general | solution.py:59
  293.7 0.0 collective-permute-done
  293.7 8.7 %broadcast_select_fusion.1 = (bf16[1,2560,1024]{2,1,0:T(8,128)(2,1)}, bf16[1,2560,1024]{2,1,0:T(8,128)(2,1)}) fusion(bf16[1,2560,1024]{2,1,0:T(8,128)(2,1)} %collective-permute-done, pred[]{:T(512)S(6)} %eq.26, bf16[2560,1024]{1,0:T(8,128)(2,1)} %param.11), kind=kLoop, calls=%fused_computation.12 | loop fusion | flops 5242880 | bytes 20971520 | tf_op jit(solution)/shard_map/jit(_where)/select_n | solution.py:22
  302.4 31.5 %all-gather.6.cloned.1.call-done = bf16[5120,1024]{1,0:T(8,128)(2,1)} async-done(((bf16[2560,1024]{1,0:T(8,128)(2,1)}), bf16[5120,1024]{1,0:T(8,128)(2,1)}) %all-gather.6.cloned.1.call-update) | async-done | bytes 10485776 | tf_op jit(solution)/shard_map/all_gather | solution.py:55
  333.9 0.0 copy-start
  333.9 0.0 copy-start.1
  333.9 6.5 %fusion.34 = f32[256,1024]{1,0:T(8,128)S(1)} fusion(bf16[256,5120]{0,1:T(8,128)(2,1)} %fusion.7, bf16[5120,1024]{1,0:T(8,128)(2,1)} %all-gather.6.cloned.1.call-done), kind=kOutput, calls=%fused_computation.27 | convolution fusion | flops 2684354560 | bytes 14155776 | tf_op jit(solution)/shard_map/dot_general | solution.py:59
  340.5 0.0 copy-done
  340.5 1.3 copy-done.1
  341.8 3.9 %fusion.28 = bf16[256,1024]{1,0:T(8,128)(2,1)} fusion(bf16[1,2560,1024]{2,1,0:T(8,128)(2,1)S(1)} %copy-done.1, bf16[1,2560,1024]{2,1,0:T(8,128)(2,1)S(1)} %copy-done, bf16[2,256,2560]{1,2,0:T(8,128)(2,1)S(1)} %all-to-all-done, f32[2,2560]{1,0:T(2,128)S(1)} %mul.56, f32[256]{0:T(256)S(1)} %add_rsqrt_fusion, f32[256,1024]{1,0:T(8,128)S(1)} %fusion.34), kind=kOutput, calls=%fused_computation.22 | convolution fusion | flops 2696413184 | bytes 14701568 | tf_op jit(solution)/shard_map/dot_general | solution.py:59
  (3 shorter events, 0.0 us)
Async XLA Ops:
  8.0 123.4 %all-reduce.2.cloned.1.call-start = ((), (), s32[]{:S(2)}) async-start(), calls=%async_computation.1 | async-start | bytes 5242880 | tf_op jit(solution)/shard_map/psum | solution.py:48
  28.7 259.8 %all-gather.4.cloned.1.call-start = ((), (), s32[]{:S(2)}) async-start(), calls=%async_computation.2 | async-start | bytes 6881280 | tf_op jit(solution)/shard_map/all_gather | solution.py:54
  29.3 106.1 %copy-start.2 = (f32[5120]{0:T(1024)S(1)}, f32[5120]{0:T(1024)}, u32[]{:S(2)}) copy-start(f32[5120]{0:T(1024)} %param.8) | copy-start | bytes 61444
  29.3 304.6 %all-gather.6.cloned.1.call-start = ((), (), s32[]{:S(2)}) async-start(), calls=%async_computation.3 | async-start | bytes 15728640 | tf_op jit(solution)/shard_map/all_gather | solution.py:55
  29.9 263.8 %collective-permute-start = (bf16[1,2560,1024]{2,1,0:T(8,128)(2,1)}, bf16[1,2560,1024]{2,1,0:T(8,128)(2,1)}, u32[]{:S(2)}, u32[]{:S(2)}) collective-permute-start(bf16[1,2560,1024]{2,1,0:T(8,128)(2,1)} %bitcast.34), channel_id=1, source_target_pairs={{0,1},{1,0},{2,3},{3,2},{4,5},{5,4},{6,7},{7,6},{8,9},{9,8},{10,11... | collective-permute-start | bytes 15728648 | tf_op jit(solution)/shard_map/ppermute | solution.py:20
  131.4 153.1 %all-to-all-start = ((bf16[2,256,2560]{1,2,0:T(8,128)(2,1)}), bf16[2,256,2560]{1,2,0:T(8,128)(2,1)S(1)}, u32[]{:S(2)}, u32[]{:S(2)}) async-start(bf16[2,256,2560]{1,2,0:T(8,128)(2,1)} %all-reduce.2.cloned.1.call-done), calls=%async_computation | async-start | bytes 5242880 | tf_op jit(solution)/shard_map/all_to_all | solution.py:49
  333.9 6.6 %copy-start = (bf16[1,2560,1024]{2,1,0:T(8,128)(2,1)S(1)}, bf16[1,2560,1024]{2,1,0:T(8,128)(2,1)}, u32[]{:S(2)}) copy-start(bf16[1,2560,1024]{2,1,0:T(8,128)(2,1)} %get-tuple-element.12) | copy-start | bytes 15728644
  333.9 7.8 %copy-start.1 = (bf16[1,2560,1024]{2,1,0:T(8,128)(2,1)S(1)}, bf16[1,2560,1024]{2,1,0:T(8,128)(2,1)}, u32[]{:S(2)}) copy-start(bf16[1,2560,1024]{2,1,0:T(8,128)(2,1)} %get-tuple-element.13) | copy-start | bytes 15728644
Sparse Core Ops, SparseCore 0:
  28.9 102.4 all-reduce.1
Sparse Core Ops, SparseCore 1:
  30.7 112.0 all-gather.3
  144.2 189.6 all-gather.5

commit v2 on v0

--- a/solution.py
+++ b/solution.py
@@ -24,7 +24,11 @@
     every_id = lax.all_gather(token_ids, "col", axis=0, tiled=True)
     vocab_rows = table.shape[0]
     partial_value = lookup_partial(every_id, table, lax.axis_index("row") * vocab_rows)
-    embedded = lax.psum(partial_value, "row").astype(jnp.float32).astype(jnp.bfloat16)
+    embedded = (
+        jnp.sum(lax.all_gather(partial_value, "row"), axis=0)
+        .astype(jnp.float32)
+        .astype(jnp.bfloat16)
+    )
     token_rows = lax.all_to_all(embedded, "col", split_axis=0, concat_axis=1, tiled=True)
     values = token_rows.astype(jnp.float32)
     factor = lax.rsqrt(jnp.mean(values * values, axis=1, keepdims=True) + eps)

time: 399 us -> 604 us (1.51)
  waiting for transfers between devices: 276 us -> 455 us
  other arithmetic: 2.91 us -> 25.8 us
    all_gather x0 -> x1, waiting for transfers between devices: none -> 207 us  [body(): lax.all_gather(partial_value, 'row')]
    psum x1 -> x0, waiting for transfers between devices: 101 us -> none  [body(): lax.psum(partial_value, 'row').astype(jnp.float32).astype(jnp.bfloat16)]
    all_gather x1, waiting for transfers between devices: 51 us -> 122 us  [body(): lax.all_gather(w_gate, 'col', axis=0, tiled=True)]
    reduce_sum x0 -> x1, other arithmetic: none -> 18.3 us  [body(): jnp.sum(lax.all_gather(partial_value, 'row'), axis=0).astype(jnp.float32)]
  transfers between devices with their start and end apart: 4 -> 4, of which waited for: 3 -> 3; matrix products, arithmetic and copies ran while one was open for 4% -> 7% of each run, Pallas kernels for 0% -> 0%
where the time goes in v2:
time: 604 us; the launch traced here: 603 us
  waiting for transfers between devices  455 us (75%)
  blocking collectives  69 us (11%)
  matrix products  33.8 us (6%)
  other arithmetic  25.8 us (4%)
  between operations  13.8 us (2%)
    all_gather x1, waiting for transfers between devices, body(): lax.all_gather(partial_value, 'row')  207 us
    all_gather x1, waiting for transfers between devices, body(): lax.all_gather(w_up, 'col', axis=0, tiled=True)  123 us
    all_gather x1, waiting for transfers between devices, body(): lax.all_gather(w_gate, 'col', axis=0, tiled=True)  122 us
    all_to_all x1, blocking collectives, body(): lax.all_to_all(embedded, 'col', split_axis=0, concat_axis=1, tiled=True)  63.5 us
    dot_general x3, matrix products, body(): jnp.dot(normed, piece, preferred_element_type=jnp.float32)  20.2 us
    reduce_sum x1, other arithmetic, body(): jnp.sum(lax.all_gather(partial_value, 'row'), axis=0).astype(jnp.float32)  18.3 us
    dot_general x1, matrix products, one_block(): jnp.dot(onehot, table_tile, preferred_element_type=jnp.float32)  13.7 us
  transfers between devices with their start and end apart: 4, of which 3 were waited for; matrix products, arithmetic and copies ran while one was open for 7% of the time, Pallas kernels for 0%

profile of v2, /device:TPU:0, one launch (start us, length us, event | category | flops | bytes accessed | tf_op | source)
XLA Modules:
  0.0 603.2 jit_solution(1444126648186632801)
XLA Ops:
  7.2 0.0 all-gather.13.cloned.1.call-start
  7.2 5.4 all-gather.1
  12.7 13.7 %fusion.5 = bf16[512,2560]{1,0:T(8,128)(2,1)} fusion(bf16[3160,2560]{1,0:T(8,128)(2,1)} %param.7, s32[3160]{0:T(1024)S(1)} %iota_add_fusion, s32[512]{0:T(512)S(1)} %bitcast.21), kind=kOutput, calls=%fused_computation.8 | convolution fusion | flops 8286679040 | bytes 18815328 | tf_op jit(solution)/shard_map/while/body/eval_jaxpr/dot_general | solution.py:17
  26.3 0.0 all-gather.13.cloned.1.call-update
  26.4 0.0 all-gather.7.cloned.1.call-start
  26.4 0.7 all-gather.7.cloned.1.call-update
  27.1 0.0 all-gather.9.cloned.1.call-start
  27.2 0.7 all-gather.9.cloned.1.call-update
  27.8 0.0 all-gather.11.cloned.1.call-start
  27.9 0.5 all-gather.11.cloned.1.call-update
  28.4 207.4 %all-gather.13.cloned.1.call-done = bf16[8192,2560]{1,0:T(8,128)(2,1)} async-done(((bf16[512,2560]{1,0:T(8,128)(2,1)}), bf16[8192,2560]{1,0:T(8,128)(2,1)}) %all-gather.13.cloned.1.call-update) | async-done | bytes 41943056 | tf_op jit(solution)/shard_map/all_gather | solution.py:28
  235.8 18.3 %reduce_sum.21 = bf16[512,2560]{1,0:T(8,128)(2,1)} reduce(bf16[16,512,2560]{2,1,0:T(8,128)(2,1)} %bitcast.19, bf16[]{:T(256)} %constant.16.clone.1), dimensions={0}, to_apply=%region_0.1 | reduce | flops 19660800 | bytes 44564480 | tf_op jit(solution)/shard_map/reduce_sum | solution.py:28
  254.1 63.5 %all_to_all.13 = bf16[2,256,2560]{2,1,0:T(8,128)(2,1)S(1)} all-to-all(bf16[2,256,2560]{2,1,0:T(8,128)(2,1)} %bitcast.20), channel_id=1, replica_groups=mesh['row'=16,'col'=2] {'col'}, dimensions={0} | all-to-all | bytes 5242880 | tf_op jit(solution)/shard_map/all_to_all | solution.py:32
  317.6 3.0 convert_bitcast_fusion
  320.6 0.0 copy-start
  320.6 5.9 copy.9
  326.6 0.6 fusion.2
  327.2 0.0 copy-done
  327.2 3.9 fusion.4
  331.1 0.0 all-gather.7.cloned.1.call-done
  331.1 4.3 convolution_convert_fusion
  335.5 122.3 %all-gather.9.cloned.1.call-done = bf16[5120,1024]{1,0:T(8,128)(2,1)} async-done(((bf16[2560,1024]{1,0:T(8,128)(2,1)}), bf16[5120,1024]{1,0:T(8,128)(2,1)}) %all-gather.9.cloned.1.call-update) | async-done | bytes 10485776 | tf_op jit(solution)/shard_map/all_gather | solution.py:38
  457.8 7.8 %fusion.11 = f32[256,1024]{1,0:T(8,128)} fusion(bf16[256,5120]{0,1:T(8,128)(2,1)S(1)} %fusion.4, bf16[5120,1024]{1,0:T(8,128)(2,1)} %all-gather.9.cloned.1.call-done), kind=kOutput, calls=%fused_computation.16 | convolution fusion | flops 2684354560 | bytes 14155776 | tf_op jit(solution)/shard_map/dot_general | solution.py:42
  465.6 123.1 %all-gather.11.cloned.1.call-done = bf16[5120,1024]{1,0:T(8,128)(2,1)} async-done(((bf16[2560,1024]{1,0:T(8,128)(2,1)}), bf16[5120,1024]{1,0:T(8,128)(2,1)}) %all-gather.11.cloned.1.call-update) | async-done | bytes 10485776 | tf_op jit(solution)/shard_map/all_gather | solution.py:39
  588.7 8.0 %fusion.10 = bf16[256,1024]{1,0:T(8,128)(2,1)} fusion(bf16[256,5120]{0,1:T(8,128)(2,1)S(1)} %fusion.4, bf16[5120,1024]{1,0:T(8,128)(2,1)} %all-gather.11.cloned.1.call-done, f32[256,1024]{1,0:T(8,128)} %fusion.11), kind=kOutput, calls=%fused_computation.12 | convolution fusion | flops 2685927424 | bytes 14680064 | tf_op jit(solution)/shard_map/dot_general | solution.py:42
  (2 shorter events, 0.0 us)
Async XLA Ops:
  7.2 228.6 %all-gather.13.cloned.1.call-start = ((), (), s32[]{:S(2)}) async-start(), calls=%async_computation.4 | async-start | bytes 44564480 | tf_op jit(solution)/shard_map/all_gather | solution.py:28
  26.4 304.8 %all-gather.7.cloned.1.call-start = ((), (), s32[]{:S(2)}) async-start(), calls=%async_computation.1 | async-start | bytes 6881280 | tf_op jit(solution)/shard_map/all_gather | solution.py:37
  27.1 430.6 %all-gather.9.cloned.1.call-start = ((), (), s32[]{:S(2)}) async-start(), calls=%async_computation.2 | async-start | bytes 15728640 | tf_op jit(solution)/shard_map/all_gather | solution.py:38
  27.8 560.9 %all-gather.11.cloned.1.call-start = ((), (), s32[]{:S(2)}) async-start(), calls=%async_computation.3 | async-start | bytes 15728640 | tf_op jit(solution)/shard_map/all_gather | solution.py:39
  320.6 6.6 %copy-start = (f32[5120]{0:T(1024)S(1)}, f32[5120]{0:T(1024)}, u32[]{:S(2)}) copy-start(f32[5120]{0:T(1024)} %param.8) | copy-start | bytes 61444
Sparse Core Ops, SparseCore 0:
  26.5 209.2 all-gather.12
  237.3 89.2 all-gather.6
  328.2 129.5 all-gather.8
  459.2 129.5 all-gather.10
